TPU v7x, 32 devices: a whole 2x2x4 slice. The times are simulated.
32 devices in a mesh: ctx: 4 (over y, core), tp: 4 (over z), dp: 2 (over x).
Axes of the slice: x: 2, y: 2, z: 4, core: 2. Of those that a mesh axis runs over, the one named last changes fastest.
Arguments:
- tokens: bfloat16 [3072, 3584], P(('dp', 'ctx'), 'tp'), may hold values from -6 to 6
- expert_ids: int32 [3072, 8], P(('dp', 'ctx')), may hold values from 0 to 255, all different within a row; in each aligned block of 384 rows (0 to 383, 384 to 767, ...) at most 24 rows name the same one
- gate_codes: int32 [3072, 8], P(('dp', 'ctx')), may hold values from 1 to 32767
- up_weight: bfloat16 [4, 3584, 1024], P('ctx', 'tp', 'dp'), may hold values from -0.09375 to 0.09375
- down_weight: bfloat16 [4, 1024, 3584], P('ctx', 'dp', 'tp'), may hold values from -0.1875 to 0.1875
- cotangent: bfloat16 [3072, 3584], P(('dp', 'ctx'), 'tp'), may hold values from -6 to 6
Outputs:
- mixed: bfloat16 [3072, 3584], P(('dp', 'ctx'), 'tp')
- grad_tokens: bfloat16 [3072, 3584], P(('dp', 'ctx'), 'tp')
- grad_up: bfloat16 [4, 3584, 1024], P('ctx', 'tp', 'dp')
- grad_down: bfloat16 [4, 1024, 3584], P('ctx', 'dp', 'tp')
Inputs may be any that keep to these rules, and one draw needn't show every extreme that they name: `expert_ids`: each row names 8 different experts; among the 384 rows of one device no expert is named more than 24 times.
All inputs are finite; a program needn't handle non-finite values.
Results may differ from a plain program's by a relative error of at most 0.0066.
Values may be sent and summed in bfloat16 or wider, within the bound.
A program may use at most 64 MiB of HBM per device.

v0:
```python
import jax
import jax.numpy as jnp
from jax import lax
from jax.sharding import PartitionSpec as P


def place_slots(expert_ids, gate_codes, experts, capacity):
    rows_count, picks = expert_ids.shape
    flat_ids = expert_ids.reshape(-1)
    one_hot = (flat_ids[:, None] == jnp.arange(experts, dtype=jnp.int32)[None, :]).astype(jnp.int32)
    before = jnp.cumsum(one_hot, axis=0) - one_hot
    slot_rank = jnp.sum(before * one_hot, axis=1)
    inside = flat_ids < experts
    target = jnp.where(inside, flat_ids * capacity + slot_rank, experts * capacity)
    source = jnp.arange(rows_count * picks, dtype=jnp.int32) // picks
    slot_token = (
        jnp.full((experts * capacity,), rows_count, jnp.int32).at[target].set(source, mode="drop")
    )
    weights = gate_codes.reshape(-1).astype(jnp.float32) / 32768.0
    gate_slot = jnp.zeros((experts * capacity,), jnp.float32).at[target].set(weights, mode="drop")
    return (slot_token, gate_slot)


def silu_grad(values):
    sigma = jax.nn.sigmoid(values)
    return sigma * (1.0 + values * (1.0 - sigma))


def body(tokens, expert_ids, gate_codes, up_weight, down_weight, cotangent):
    sources = lax.axis_size("ctx")
    rows_count, features = tokens.shape
    capacity = rows_count // 16
    slot_token, gate_slot = place_slots(expert_ids, gate_codes, sources, capacity)
    padded_x = jnp.concatenate([tokens, jnp.zeros((1, features), tokens.dtype)], axis=0)
    outgoing = padded_x[slot_token].reshape(sources, capacity, features)
    arrived = lax.all_to_all(outgoing, "ctx", split_axis=0, concat_axis=0, tiled=True).reshape(
        sources * capacity, features
    )
    w_up, w_down = (
        lax.all_gather(up_weight[0], "dp", axis=1, tiled=True),
        lax.all_gather(down_weight[0], "dp", axis=0, tiled=True),
    )
    hidden = lax.psum(jnp.dot(arrived, w_up, preferred_element_type=jnp.float32), "tp")
    active = jax.nn.silu(hidden).astype(jnp.bfloat16)
    produced = jnp.dot(active, w_down, preferred_element_type=jnp.float32).astype(jnp.bfloat16)
    returned = lax.all_to_all(
        produced.reshape(sources, capacity, features),
        "ctx",
        split_axis=0,
        concat_axis=0,
        tiled=True,
    ).reshape(sources * capacity, features)
    mixed = (
        jnp.zeros((rows_count + 1, features), jnp.float32)
        .at[slot_token]
        .add(gate_slot[:, None] * returned.astype(jnp.float32))
    )
    mixed = mixed[:rows_count].astype(jnp.bfloat16)
    padded_c = jnp.concatenate([cotangent, jnp.zeros((1, features), cotangent.dtype)], axis=0)
    grad_send = (gate_slot[:, None] * padded_c[slot_token].astype(jnp.float32)).astype(jnp.bfloat16)
    grad_rows = lax.all_to_all(
        grad_send.reshape(sources, capacity, features),
        "ctx",
        split_axis=0,
        concat_axis=0,
        tiled=True,
    ).reshape(sources * capacity, features)
    contract_last = (((1,), (1,)), ((), ()))
    contract_first = (((0,), (0,)), ((), ()))
    grad_act = lax.psum(
        lax.dot_general(grad_rows, w_down, contract_last, preferred_element_type=jnp.float32), "tp"
    )
    grad_hid = (grad_act * silu_grad(hidden)).astype(jnp.bfloat16)
    grad_in = lax.dot_general(
        grad_hid, w_up, contract_last, preferred_element_type=jnp.float32
    ).astype(jnp.bfloat16)
    back_rows = lax.all_to_all(
        grad_in.reshape(sources, capacity, features), "ctx", split_axis=0, concat_axis=0, tiled=True
    ).reshape(sources * capacity, features)
    grad_tokens = (
        jnp.zeros((rows_count + 1, features), jnp.float32)
        .at[slot_token]
        .add(back_rows.astype(jnp.float32))
    )
    grad_tokens = grad_tokens[:rows_count].astype(jnp.bfloat16)
    part_up = lax.dot_general(arrived, grad_hid, contract_first, preferred_element_type=jnp.float32)
    part_down = lax.dot_general(
        active, grad_rows, contract_first, preferred_element_type=jnp.float32
    )
    grad_up, grad_down = (
        lax.psum_scatter(
            part_up.astype(jnp.bfloat16), "dp", scatter_dimension=1, tiled=True
        ).astype(jnp.float32),
        lax.psum_scatter(
            part_down.astype(jnp.bfloat16), "dp", scatter_dimension=0, tiled=True
        ).astype(jnp.float32),
    )
    return (
        mixed,
        grad_tokens,
        grad_up.astype(jnp.bfloat16)[None],
        grad_down.astype(jnp.bfloat16)[None],
    )


def solution(mesh):
    return jax.shard_map(
        body,
        mesh=mesh,
        in_specs=(
            P(("dp", "ctx"), "tp"),
            P(("dp", "ctx"), None),
            P(("dp", "ctx"), None),
            P("ctx", "tp", "dp"),
            P("ctx", "dp", "tp"),
            P(("dp", "ctx"), "tp"),
        ),
        out_specs=(
            P(("dp", "ctx"), "tp"),
            P(("dp", "ctx"), "tp"),
            P("ctx", "tp", "dp"),
            P("ctx", "dp", "tp"),
        ),
        check_vma=False,
    )
```

profile of v0, /device:TPU:1, one launch (start us, length us, event | category | flops | bytes accessed | tf_op | source)
XLA Modules:
  0.0 190.0 jit_solution(14327130908680088390)
XLA Ops:
  7.2 0.0 copy-start.5
  7.2 0.0 copy-start.2
  7.2 0.0 all-gather.5.cloned.1.call-start
  7.2 0.7 all-gather.5.cloned.1.call-update
  7.9 0.0 all-gather.7.cloned.1.call-start
  8.0 0.7 all-gather.7.cloned.1.call-update
  8.7 0.0 copy-done.5
  8.7 0.1 copy.12
  8.8 0.1 eq.29
  9.0 0.1 eq.25
  9.1 0.2 copy.10
  9.3 0.2 lt.35
  9.4 0.1 copy.11
  9.6 0.1 mul.53
  9.7 0.0 copy-start.6
  9.7 1.2 reduce-window.6
  10.9 0.2 slice_reduce_fusion
  11.1 0.2 reduce-window.9
  11.3 0.1 add_bitcast_fusion
  11.5 0.0 copy-done.2
  11.5 0.0 copy-start.3
  11.5 0.1 concatenate.6
  11.6 11.8 %scatter_custom_fusion = s32[96]{0:T(128)S(1)} fusion(s32[3072]{0:T(1024)S(1)} %bitcast.64, s32[3072]{0:T(1024)S(1)} %add_select_fusion, s32[]{:T(128)} %constant.17.clone.1), kind=kCustom, calls=%fused_computation.56 | custom fusion | bytes 388 | tf_op jit(solution)/shard_map/scatter | solution.py:17
  23.4 1.5 gather_fusion
  24.9 4.3 %all-to-all-start = ((bf16[4,24,896]{2,1,0:T(8,128)(2,1)}), bf16[4,24,896]{2,1,0:T(8,128)(2,1)S(1)}, u32[]{:S(2)}, u32[]{:S(2)}) async-start(bf16[4,24,896]{2,1,0:T(8,128)(2,1)} %bitcast.3), calls=%async_computation | async-start | bytes 344064 | tf_op jit(solution)/shard_map/all_to_all | solution.py:36
  29.1 0.0 copy-done.6
  29.1 0.1 copy.14
  29.3 0.1 reshape.139
  29.4 11.8 %scatter_custom_fusion.1 = f32[96]{0:T(128)S(1)} fusion(s32[3072]{0:T(1024)S(1)} %bitcast.65, f32[3072]{0:T(1024)S(1)} %reshape.139, f32[]{:T(128)} %constant.15.clone.1), kind=kCustom, calls=%fused_computation.54 | custom fusion | bytes 388 | tf_op jit(solution)/shard_map/scatter | solution.py:20
  41.2 0.1 mul.58
  41.3 0.0 copy-done.3
  41.3 0.1 concatenate.7
  41.3 0.8 gather_fusion.1
  42.1 0.8 fusion.19
  42.9 0.0 all-to-all-done
  42.9 3.4 %all-to-all-start.2 = ((bf16[4,24,896]{2,1,0:T(8,128)(2,1)}), bf16[4,24,896]{2,1,0:T(8,128)(2,1)S(1)}, u32[]{:S(2)}, u32[]{:S(2)}) async-start(bf16[4,24,896]{2,1,0:T(8,128)(2,1)} %fusion.19), calls=%async_computation.2 | async-start | bytes 344064 | tf_op jit(solution)/shard_map/all_to_all | solution.py:61
  46.3 0.0 all-reduce.5.cloned.1.call-start
  46.3 0.0 all-gather.5.cloned.1.call-done
  46.3 2.7 %fusion.6 = f32[96,1024]{1,0:T(8,128)} fusion(bf16[96,896]{1,0:T(8,128)(2,1)S(1)} %bitcast.56, bf16[1,896,1024]{2,1,0:T(8,128)(2,1)} %all-gather.5.cloned.1.call-done), kind=kOutput, calls=%fused_computation.12 | convolution fusion | flops 176160768 | bytes 2400256 | tf_op jit(solution)/shard_map/dot_general | solution.py:43
  49.0 1.1 all-to-all-done.2
  50.2 23.2 %all-gather.7.cloned.1.call-done = bf16[1,1024,896]{2,1,0:T(8,128)(2,1)} async-done(((bf16[1,512,896]{2,1,0:T(8,128)(2,1)}), bf16[1,1024,896]{2,1,0:T(8,128)(2,1)}) %all-gather.7.cloned.1.call-update) | async-done | bytes 1835024 | tf_op jit(solution)/shard_map/all_gather | solution.py:41
  73.3 2.9 %fusion = f32[96,1024]{1,0:T(8,128)} fusion(bf16[96,896]{1,0:T(8,128)(2,1)S(1)} %bitcast.58, bf16[1,1024,896]{2,1,0:T(8,128)(2,1)} %all-gather.7.cloned.1.call-done), kind=kOutput, calls=%fused_computation.6 | convolution fusion | flops 176160768 | bytes 2400256 | tf_op jit(solution)/shard_map/dot_general | solution.py:71
  76.3 0.0 all-reduce.5.cloned.1.call-update
  76.3 0.0 reduce-scatter.5.cloned.1.call-start
  76.3 43.7 %all-reduce.5.cloned.1.call-done = (f32[96,1024]{1,0:T(8,128)}, f32[96,1024]{1,0:T(8,128)}) async-done(((f32[96,1024]{1,0:T(8,128)}, f32[96,1024]{1,0:T(8,128)}), (f32[96,1024]{1,0:T(8,128)}, f32[96,1024]{1,0:T(8,128)})) %all-reduce.5.cloned.1.call-update) | async-done | bytes 786448 | tf_op jit(solution)/shard_map/psum | solution.py:43
  120.1 3.0 %convolution_convert_fusion = bf16[1024,896]{1,0:T(8,128)(2,1)} fusion(bf16[96,896]{1,0:T(8,128)(2,1)S(1)} %bitcast.59, f32[96,1024]{1,0:T(8,128)} %get-tuple-element.4), kind=kOutput, calls=%fused_computation.14 | convolution fusion | flops 177569792 | bytes 2400256 | tf_op jit(solution)/shard_map/dot_general | solution.py:87
  123.1 0.0 reduce-scatter.5.cloned.1.call-update
  123.1 0.0 reduce-scatter.3.cloned.1.call-start
  123.1 0.0 copy-done.1
  123.1 0.2 multiply_convert_fusion
  123.3 1.9 %convolution_convert_fusion.1 = bf16[896,1024]{1,0:T(8,128)(2,1)} fusion(bf16[96,896]{1,0:T(8,128)(2,1)S(1)} %bitcast.57, bf16[96,1024]{1,0:T(8,128)(2,1)S(1)} %multiply_convert_fusion), kind=kOutput, calls=%fused_computation.15 | convolution fusion | flops 177078272 | bytes 2203648 | tf_op jit(solution)/shard_map/dot_general | solution.py:86
  125.3 0.0 reduce-scatter.3.cloned.1.call-update
  125.3 2.8 %fusion.11 = bf16[96,896]{1,0:T(8,128)(2,1)} fusion(bf16[1,1024,896]{2,1,0:T(8,128)(2,1)} %all-gather.7.cloned.1.call-done, f32[96,1024]{1,0:T(8,128)S(1)} %copy-done.1), kind=kOutput, calls=%fused_computation.19 | convolution fusion | flops 176738304 | bytes 2400256 | tf_op jit(solution)/shard_map/dot_general | solution.py:45
  128.0 4.4 %all-to-all-start.1 = ((bf16[4,24,896]{2,1,0:T(8,128)(2,1)}), bf16[4,24,896]{2,1,0:T(8,128)(2,1)S(1)}, u32[]{:S(2)}, u32[]{:S(2)}) async-start(bf16[4,24,896]{2,1,0:T(8,128)(2,1)} %bitcast.7), calls=%async_computation.1 | async-start | bytes 344064 | tf_op jit(solution)/shard_map/all_to_all | solution.py:46
  132.5 1.3 fusion.8
  133.8 3.0 %all-to-all-done.1 = bf16[4,24,896]{2,1,0:T(8,128)(2,1)S(1)} async-done(((bf16[4,24,896]{2,1,0:T(8,128)(2,1)}), bf16[4,24,896]{2,1,0:T(8,128)(2,1)S(1)}, u32[]{:S(2)}, u32[]{:S(2)}) %all-to-all-start.1) | async-done | bytes 172064 | tf_op jit(solution)/shard_map/all_to_all | solution.py:46
  136.8 4.1 %all-to-all-start.3 = ((bf16[4,24,896]{2,1,0:T(8,128)(2,1)}), bf16[4,24,896]{2,1,0:T(8,128)(2,1)S(1)}, u32[]{:S(2)}, u32[]{:S(2)}) async-start(bf16[4,24,896]{2,1,0:T(8,128)(2,1)} %bitcast.11), calls=%async_computation.3 | async-start | bytes 344064 | tf_op jit(solution)/shard_map/all_to_all | solution.py:77
  140.8 1.8 scatter_custom_fusion.2
  142.6 0.9 slice.29
  143.5 1.6 all-to-all-done.3
  145.1 1.7 scatter_custom_fusion.3
  146.8 0.9 slice.28
  147.8 4.0 %reduce-scatter.5.cloned.1.call-done = bf16[512,896]{1,0:T(8,128)(2,1)} async-done(((bf16[1024,896]{1,0:T(8,128)(2,1)}), bf16[512,896]{1,0:T(8,128)(2,1)}) %reduce-scatter.5.cloned.1.call-update) | async-done | bytes 917520 | tf_op jit(solution)/shard_map/reduce_scatter | solution.py:94
  151.7 31.7 %reduce-scatter.3.cloned.1.call-done = bf16[896,512]{1,0:T(8,128)(2,1)} async-done(((bf16[896,1024]{1,0:T(8,128)(2,1)}), bf16[896,512]{1,0:T(8,128)(2,1)}) %reduce-scatter.3.cloned.1.call-update) | async-done | bytes 917520 | tf_op jit(solution)/shard_map/reduce_scatter | solution.py:91
  (14 shorter events, 0.1 us)
Async XLA Ops:
  7.2 1.5 copy-start.5
  7.2 4.3 %copy-start.2 = (bf16[384,896]{1,0:T(8,128)(2,1)S(1)}, bf16[384,896]{1,0:T(8,128)(2,1)}, u32[]{:S(2)}) copy-start(bf16[384,896]{1,0:T(8,128)(2,1)} %param.6) | copy-start | bytes 2064388
  7.2 39.1 %all-gather.5.cloned.1.call-start = ((), (), s32[]{:S(2)}) async-start(), calls=%async_computation.8 | async-start | bytes 2752512 | tf_op jit(solution)/shard_map/all_gather | solution.py:40
  7.9 65.4 %all-gather.7.cloned.1.call-start = ((), (), s32[]{:S(2)}) async-start(), calls=%async_computation.9 | async-start | bytes 2752512 | tf_op jit(solution)/shard_map/all_gather | solution.py:41
  9.7 19.4 %copy-start.6 = (s32[384,8]{0,1:T(8,128)S(1)}, s32[384,8]{0,1:T(8,128)}, u32[]{:S(2)}) copy-start(s32[384,8]{0,1:T(8,128)} %param.8) | copy-start | bytes 36868
  11.5 29.8 %copy-start.3 = (bf16[384,896]{1,0:T(8,128)(2,1)S(1)}, bf16[384,896]{1,0:T(8,128)(2,1)}, u32[]{:S(2)}) copy-start(bf16[384,896]{1,0:T(8,128)(2,1)} %param.11) | copy-start | bytes 2064388
  24.9 18.1 %all-to-all-start = ((bf16[4,24,896]{2,1,0:T(8,128)(2,1)}), bf16[4,24,896]{2,1,0:T(8,128)(2,1)S(1)}, u32[]{:S(2)}, u32[]{:S(2)}) async-start(bf16[4,24,896]{2,1,0:T(8,128)(2,1)} %bitcast.3), calls=%async_computation | async-start | bytes 344064 | tf_op jit(solution)/shard_map/all_to_all | solution.py:36
  42.9 7.3 %all-to-all-start.2 = ((bf16[4,24,896]{2,1,0:T(8,128)(2,1)}), bf16[4,24,896]{2,1,0:T(8,128)(2,1)S(1)}, u32[]{:S(2)}, u32[]{:S(2)}) async-start(bf16[4,24,896]{2,1,0:T(8,128)(2,1)} %fusion.19), calls=%async_computation.2 | async-start | bytes 344064 | tf_op jit(solution)/shard_map/all_to_all | solution.py:61
  46.3 73.8 %all-reduce.5.cloned.1.call-start = ((), (), s32[]{:S(2)}) async-start(), calls=%async_computation.10 | async-start | bytes 1572864 | tf_op jit(solution)/shard_map/psum | solution.py:43
  76.3 75.5 %reduce-scatter.5.cloned.1.call-start = ((), (), s32[]{:S(2)}) async-start(), calls=%async_computation.7 | async-start | bytes 2752512 | tf_op jit(solution)/shard_map/reduce_scatter | solution.py:94
  120.1 3.1 %copy-start.1 = (f32[96,1024]{1,0:T(8,128)S(1)}, f32[96,1024]{1,0:T(8,128)}, u32[]{:S(2)}) copy-start(f32[96,1024]{1,0:T(8,128)} %get-tuple-element.4) | copy-start | bytes 1179652
  120.1 3.1 %copy-start.4 = (f32[96,1024]{1,0:T(8,128)S(1)}, f32[96,1024]{1,0:T(8,128)}, u32[]{:S(2)}) copy-start(f32[96,1024]{1,0:T(8,128)} %get-tuple-element.5) | copy-start | bytes 1179652
  123.1 60.4 %reduce-scatter.3.cloned.1.call-start = ((), (), s32[]{:S(2)}) async-start(), calls=%async_computation.6 | async-start | bytes 2752512 | tf_op jit(solution)/shard_map/reduce_scatter | solution.py:91
  125.3 7.2 %copy-start = (bf16[1,896,1024]{2,1,0:T(8,128)(2,1)S(1)}, bf16[1,896,1024]{2,1,0:T(8,128)(2,1)}, u32[]{:S(2)}) copy-start(bf16[1,896,1024]{2,1,0:T(8,128)(2,1)} %all-gather.5.cloned.1.call-done) | copy-start | bytes 5505028
  128.0 8.7 %all-to-all-start.1 = ((bf16[4,24,896]{2,1,0:T(8,128)(2,1)}), bf16[4,24,896]{2,1,0:T(8,128)(2,1)S(1)}, u32[]{:S(2)}, u32[]{:S(2)}) async-start(bf16[4,24,896]{2,1,0:T(8,128)(2,1)} %bitcast.7), calls=%async_computation.1 | async-start | bytes 344064 | tf_op jit(solution)/shard_map/all_to_all | solution.py:46
  136.8 8.4 %all-to-all-start.3 = ((bf16[4,24,896]{2,1,0:T(8,128)(2,1)}), bf16[4,24,896]{2,1,0:T(8,128)(2,1)S(1)}, u32[]{:S(2)}, u32[]{:S(2)}) async-start(bf16[4,24,896]{2,1,0:T(8,128)(2,1)} %bitcast.11), calls=%async_computation.3 | async-start | bytes 344064 | tf_op jit(solution)/shard_map/all_to_all | solution.py:77
Sparse Core Ops, SparseCore 0:
  9.5 32.0 all-gather.4
  43.2 30.1 all-gather.6
  76.4 43.6 all-reduce.4
  123.2 28.4 reduce-scatter.4
  154.4 28.9 reduce-scatter.2
where the time goes:
time: 191 us; the launch traced here: 190 us
  waiting for transfers between devices  110 us (58%)
  local copies, waits for them, and re-layouts  29.3 us (15%)
  starting transfers between devices  16.3 us (9%)
  matrix products  14.6 us (8%)
  between operations  14 us (7%)
  other arithmetic  5.96 us (3%)
    psum x1, waiting for transfers between devices, body(): lax.psum(jnp.dot(arrived, w_up, preferred_element_type=jnp.float32), 'tp')  43.7 us
    reduce_scatter x1, waiting for transfers between devices, body(): lax.psum_scatter(part_up.astype(jnp.bfloat16), 'dp', scatter_dimension=1,...  31.7 us
    all_gather x1, waiting for transfers between devices, body(): lax.all_gather(down_weight[0], 'dp', axis=0, tiled=True)  23.2 us
    scatter x1, local copies, waits for them, and re-layouts, place_slots(): jnp.full((experts * capacity,), rows_count, jnp.int32).at[target]  11.8 us
    scatter x1, local copies, waits for them, and re-layouts, place_slots(): jnp.zeros((experts * capacity,), jnp.float32).at[target]  11.8 us
    all_to_all x1, starting transfers between devices, body(): lax.all_to_all(produced.reshape(sources, capacity, features), 'ctx', spli...  4.42 us
    all_to_all x1, starting transfers between devices, body(): lax.all_to_all(outgoing, 'ctx', split_axis=0, concat_axis=0, tiled=True)  4.28 us
    all_to_all x1, starting transfers between devices, body(): lax.all_to_all(grad_in.reshape(sources, capacity, features), 'ctx', split...  4.07 us
  transfers between devices with their start and end apart: 9, of which 7 were waited for; matrix products, arithmetic and copies ran while one was open for 23% of the time, Pallas kernels for 0%

commit v1 on v0

v1 whole, which is shorter than its diff:
```python
import functools

import jax
import jax.numpy as jnp
from jax import lax
from jax.experimental import pallas as pl
from jax.experimental.pallas import tpu as pltpu
from jax.sharding import PartitionSpec as P

MESH = pl.DeviceIdType.MESH
F32 = jnp.float32
BF16 = jnp.bfloat16
FIRST = (((0,), (0,)), ((), ()))
LAST = (((1,), (1,)), ((), ()))
PLAIN = (((1,), (0,)), ((), ()))


def dot(a, b, how=PLAIN):
    return lax.dot_general(a, b, how, preferred_element_type=F32)


def kernel(
    n_dp, n_ctx, n_tp, cap,
    ids_ref, codes_ref, tok_hbm, cot_hbm, up_hbm, down_hbm,
    mixed_hbm, gtok_hbm, gup_hbm, gdown_hbm,
    tok, cot, up, down, x_send, g_send, x_recv, g_recv, x_all, g_all,
    h_send, a_send, h_recv, a_recv, act, ghid,
    p_send, q_send, p_recv, q_recv, mixed, gtok, gup, gdown,
    in_sem, out_sem, xs, xr, gs, gr, hs, hr, as_, ar, cs, cr, ds, dr, ps, pr, qs, qr,
):
    d, c, t = lax.axis_index("dp"), lax.axis_index("ctx"), lax.axis_index("tp")
    n_blocks = n_dp * n_ctx
    me = d * n_ctx + c
    slots = n_ctx * cap

    loads = [
        pltpu.make_async_copy(src, dst, in_sem.at[i])
        for i, (src, dst) in enumerate(
            ((tok_hbm, tok), (cot_hbm, cot), (up_hbm.at[0], up), (down_hbm.at[0], down))
        )
    ]
    for load in loads:
        load.start()

    def block_dev(k):
        b = lax.rem(me + k, n_blocks)
        return b, {"dp": b // n_ctx, "ctx": lax.rem(b, n_ctx)}

    def tp_dev(k):
        j = lax.rem(t + k, n_tp)
        return j, {"tp": j}

    barrier = pltpu.get_barrier_semaphore()
    for k in range(1, n_blocks):
        pl.semaphore_signal(barrier, inc=1, device_id=block_dev(k)[1], device_id_type=MESH)
    for k in range(1, n_tp):
        pl.semaphore_signal(barrier, inc=1, device_id=tp_dev(k)[1], device_id_type=MESH)

    picks, rows = ids_ref.shape
    lane = lax.broadcasted_iota(jnp.int32, (slots, rows), 0)
    lane_e = jnp.zeros((slots, rows), jnp.int32)
    for e in range(1, n_ctx):
        lane_e = lane_e + (lane >= e * cap).astype(jnp.int32)
    lane_s = lane - lane_e * cap
    named = jnp.zeros((slots, rows), jnp.int32)
    code = jnp.zeros((slots, rows), jnp.int32)
    ids, codes = ids_ref[...], codes_ref[...]
    for k in range(picks):
        hit = ids[k : k + 1] == lane_e
        named = jnp.where(hit, 1, named)
        code = jnp.where(hit, codes[k : k + 1], code)
    earlier = (
        lax.broadcasted_iota(jnp.int32, (rows, rows), 0)
        < lax.broadcasted_iota(jnp.int32, (rows, rows), 1)
    )
    rank = dot(named.astype(F32).astype(BF16), earlier.astype(F32).astype(BF16))
    chosen = jnp.where(rank == lane_s.astype(F32), named, 0)
    code = chosen * code
    pick = chosen.astype(F32).astype(BF16)
    high = lax.shift_right_logical(code, 8)
    gate_hi = (high.astype(F32) * (1.0 / 128.0)).astype(BF16)
    gate_lo = ((code - high * 256).astype(F32) * (1.0 / 32768.0)).astype(BF16)

    pl.semaphore_wait(barrier, n_blocks - 1 + n_tp - 1)

    def spread(send, recv, send_sem, recv_sem):
        for k in range(1, n_blocks):
            b, dev = block_dev(k)
            pltpu.make_async_remote_copy(
                send.at[lax.rem(b, n_ctx)], recv.at[me], send_sem.at[k], recv_sem.at[me],
                device_id=dev, device_id_type=MESH,
            ).start()
        recv[me] = send[c]

    def arrived(recv, send_sem, recv_sem):
        for k in range(1, n_blocks):
            b, dev = block_dev(k)
            pltpu.make_async_remote_copy(
                recv.at[b], recv.at[b], send_sem.at[k], recv_sem.at[b],
                device_id=dev, device_id_type=MESH,
            ).wait_recv()

    def sent(send, send_sem):
        for k in range(1, n_blocks):
            b, dev = block_dev(k)
            pltpu.make_async_remote_copy(
                send.at[0], send.at[0], send_sem.at[k], send_sem.at[k],
                device_id=dev, device_id_type=MESH,
            ).wait_send()

    def put_blocks(ref, value, count):
        for b in range(count):
            ref[b] = value[b * cap : (b + 1) * cap].astype(BF16)

    def take_blocks(ref, count):
        return jnp.concatenate([ref[b].astype(F32) for b in range(count)], axis=0).astype(BF16)

    def tp_scatter(send, recv, send_sem, recv_sem):
        for k in range(1, n_tp):
            j, dev = tp_dev(k)
            pltpu.make_async_remote_copy(
                send.at[j], recv.at[t], send_sem.at[k], recv_sem.at[t],
                device_id=dev, device_id_type=MESH,
            ).start()

    def tp_gather(buf, send_sem, recv_sem):
        for k in range(1, n_tp):
            j, dev = tp_dev(k)
            pltpu.make_async_remote_copy(
                buf.at[t], buf.at[t], send_sem.at[k], recv_sem.at[t],
                device_id=dev, device_id_type=MESH,
            ).start()

    def tp_arrived(buf, send_sem, recv_sem):
        for k in range(1, n_tp):
            j, dev = tp_dev(k)
            pltpu.make_async_remote_copy(
                buf.at[j], buf.at[j], send_sem.at[k], recv_sem.at[j],
                device_id=dev, device_id_type=MESH,
            ).wait_recv()

    def tp_sent(buf, send_sem):
        for k in range(1, n_tp):
            j, dev = tp_dev(k)
            pltpu.make_async_remote_copy(
                buf.at[0], buf.at[0], send_sem.at[k], send_sem.at[k],
                device_id=dev, device_id_type=MESH,
            ).wait_send()

    loads[0].wait()
    put_blocks(x_send, dot(pick, tok[...]), n_ctx)
    spread(x_send, x_recv, xs, xr)
    loads[1].wait()
    put_blocks(g_send, dot(gate_hi, cot[...]) + dot(gate_lo, cot[...]), n_ctx)
    spread(g_send, g_recv, gs, gr)

    loads[2].wait()
    arrived(x_recv, xs, xr)
    x_all[...] = take_blocks(x_recv, n_blocks)
    piece = n_blocks * cap // n_tp
    part = dot(x_all[...], up[...])
    for j in range(n_tp):
        h_send[j] = part[j * piece : (j + 1) * piece].astype(BF16)
    tp_scatter(h_send, h_recv, hs, hr)
    loads[3].wait()
    arrived(g_recv, gs, gr)
    g_all[...] = take_blocks(g_recv, n_blocks)
    part = dot(g_all[...], down[...], LAST)
    for j in range(n_tp):
        a_send[j] = part[j * piece : (j + 1) * piece].astype(BF16)
    tp_scatter(a_send, a_recv, as_, ar)

    tp_arrived(h_recv, hs, hr)
    hidden = h_send[t].astype(F32)
    for k in range(1, n_tp):
        hidden = hidden + h_recv[lax.rem(t + k, n_tp)].astype(F32)
    sigma = 1.0 / (1.0 + jnp.exp(-hidden))
    act[t] = (hidden * sigma).astype(BF16)
    tp_gather(act, cs, cr)
    slope = sigma * (1.0 + hidden * (1.0 - sigma))
    tp_arrived(a_recv, as_, ar)
    grad_act = a_send[t].astype(F32)
    for k in range(1, n_tp):
        grad_act = grad_act + a_recv[lax.rem(t + k, n_tp)].astype(F32)
    ghid[t] = (grad_act * slope).astype(BF16)
    tp_gather(ghid, ds, dr)

    def spread_back(send, recv, send_sem, recv_sem):
        for k in range(1, n_blocks):
            b, dev = block_dev(k)
            pltpu.make_async_remote_copy(
                send.at[b], recv.at[me], send_sem.at[k], recv_sem.at[me],
                device_id=dev, device_id_type=MESH,
            ).start()
        recv[me] = send[me]

    def whole(buf):
        return jnp.concatenate([buf[j] for j in range(n_tp)], axis=0)

    tp_arrived(act, cs, cr)
    act_all = whole(act)
    put_blocks(p_send, dot(act_all, down[...]), n_blocks)
    spread_back(p_send, p_recv, ps, pr)
    tp_arrived(ghid, ds, dr)
    ghid_all = whole(ghid)
    put_blocks(q_send, dot(ghid_all, up[...], LAST), n_blocks)
    spread_back(q_send, q_recv, qs, qr)

    gdown[...] = dot(act_all, g_all[...], FIRST).astype(BF16)
    stores = [pltpu.make_async_copy(gdown, gdown_hbm.at[0], out_sem.at[0])]
    stores[-1].start()
    gup[...] = dot(x_all[...], ghid_all, FIRST).astype(BF16)
    stores.append(pltpu.make_async_copy(gup, gup_hbm.at[0], out_sem.at[1]))
    stores[-1].start()

    arrived(p_recv, ps, pr)
    got = take_blocks(p_recv, n_blocks)
    mixed[...] = (
        dot(jnp.concatenate([gate_hi] * n_dp, axis=0), got, FIRST)
        + dot(jnp.concatenate([gate_lo] * n_dp, axis=0), got, FIRST)
    ).astype(BF16)
    stores.append(pltpu.make_async_copy(mixed, mixed_hbm, out_sem.at[2]))
    stores[-1].start()
    arrived(q_recv, qs, qr)
    got = take_blocks(q_recv, n_blocks)
    gtok[...] = dot(jnp.concatenate([pick] * n_dp, axis=0), got, FIRST).astype(BF16)
    stores.append(pltpu.make_async_copy(gtok, gtok_hbm, out_sem.at[3]))
    stores[-1].start()

    sent(x_send, xs)
    sent(g_send, gs)
    tp_sent(h_recv, hs)
    tp_sent(a_recv, as_)
    tp_sent(act, cs)
    tp_sent(ghid, ds)
    sent(p_send, ps)
    sent(q_send, qs)
    for store in stores:
        store.wait()


def body(n_dp, n_ctx, n_tp, tokens, expert_ids, gate_codes, up_weight, down_weight, cotangent):
    rows, feats = tokens.shape
    hid = up_weight.shape[2]
    cap = rows // 16
    blocks = n_dp * n_ctx
    total = blocks * cap
    piece = total // n_tp
    any_ = pl.BlockSpec(memory_space=pl.ANY)
    vmem = pl.BlockSpec(memory_space=pltpu.VMEM)
    dma = pltpu.SemaphoreType.DMA

    def buf(*shape):
        return pltpu.VMEM(shape, BF16)

    return pl.pallas_call(
        functools.partial(kernel, n_dp, n_ctx, n_tp, cap),
        out_shape=[
            jax.ShapeDtypeStruct(a.shape, BF16)
            for a in (tokens, tokens, up_weight, down_weight)
        ],
        in_specs=[vmem, vmem, any_, any_, any_, any_],
        out_specs=[any_] * 4,
        scratch_shapes=[
            buf(rows, feats), buf(rows, feats), buf(feats, hid), buf(hid, feats),
            buf(n_ctx, cap, feats), buf(n_ctx, cap, feats),
            buf(blocks, cap, feats), buf(blocks, cap, feats),
            buf(total, feats), buf(total, feats),
            buf(n_tp, piece, hid), buf(n_tp, piece, hid),
            buf(n_tp, piece, hid), buf(n_tp, piece, hid),
            buf(n_tp, piece, hid), buf(n_tp, piece, hid),
            buf(blocks, cap, feats), buf(blocks, cap, feats),
            buf(blocks, cap, feats), buf(blocks, cap, feats),
            buf(rows, feats), buf(rows, feats), buf(feats, hid), buf(hid, feats),
            dma((4,)), dma((4,)),
            dma((blocks,)), dma((blocks,)), dma((blocks,)), dma((blocks,)),
            dma((n_tp,)), dma((n_tp,)), dma((n_tp,)), dma((n_tp,)),
            dma((n_tp,)), dma((n_tp,)), dma((n_tp,)), dma((n_tp,)),
            dma((blocks,)), dma((blocks,)), dma((blocks,)), dma((blocks,)),
        ],
        compiler_params=pltpu.CompilerParams(collective_id=0, has_side_effects=True),
        name="expert_layer",
    )(expert_ids.T, gate_codes.T, tokens, cotangent, up_weight, down_weight)


def solution(mesh):
    sizes = [mesh.shape[name] for name in ("dp", "ctx", "tp")]
    return jax.shard_map(
        functools.partial(body, *sizes),
        mesh=mesh,
        in_specs=(
            P(("dp", "ctx"), "tp"),
            P(("dp", "ctx"), None),
            P(("dp", "ctx"), None),
            P("ctx", "tp", "dp"),
            P("ctx", "dp", "tp"),
            P(("dp", "ctx"), "tp"),
        ),
        out_specs=(
            P(("dp", "ctx"), "tp"),
            P(("dp", "ctx"), "tp"),
            P("ctx", "tp", "dp"),
            P("ctx", "dp", "tp"),
        ),
        check_vma=False,
    )
```

time: 191 us -> 45.8 us (0.24)
  waiting for transfers between devices: 110 us -> 0 us
  Pallas kernels: 0 us -> 38.6 us
  local copies, waits for them, and re-layouts: 29.3 us -> 5.93 us
  starting transfers between devices: 16.3 us -> 0 us
  matrix products: 14.6 us -> 0 us
  between operations: 14 us -> 0.65 us
  other arithmetic: 5.96 us -> 0 us
    psum x1 -> x0, waiting for transfers between devices: 43.7 us -> none  [body(): lax.psum(jnp.dot(arrived, w_up, preferred_element_type=jnp.float32), 'tp')]
    pallas_call x0 -> x1, Pallas kernels: none -> 38.6 us  [body(): pl.pallas_call(functools.partial(kernel, n_dp, n_ctx, n_tp, cap), out_sha...]
    reduce_scatter x2 -> x0, waiting for transfers between devices: 35.7 us -> none  [the longest x1 31.7 us: body(): lax.psum_scatter(part_up.astype(jnp.bfloat16), 'dp', scatter_dimension=1,...]
    scatter x2 -> x0, local copies, waits for them, and re-layouts: 23.5 us -> none  [the longest x1 11.8 us: place_slots(): jnp.full((experts * capacity,), rows_count, jnp.int32).at[target]]
    all_gather x2 -> x0, waiting for transfers between devices: 23.2 us -> none  [the longest x1 23.2 us: body(): lax.all_gather(down_weight[0], 'dp', axis=0, tiled=True)]
    all_to_all x4 -> x0, starting transfers between devices: 16.1 us -> none  [the longest x1 4.42 us: body(): lax.all_to_all(produced.reshape(sources, capacity, features), 'ctx', spli...]
    dot_general x6 -> x0, matrix products: 14.6 us -> none  [the longest x1 2.98 us: body(): lax.dot_general(active, grad_rows, contract_first, preferred_element_type...]
    unnamed x15 -> x10, local copies, waits for them, and re-layouts: 0.15 us -> 5.93 us
  transfers between devices with their start and end apart: 9 -> 0, of which waited for: 7 -> 0; matrix products, arithmetic and copies ran while one was open for 23% -> 0% of each run, Pallas kernels for 0% -> 0%
where the time goes in v1:
time: 45.8 us; the launch traced here: 45.2 us
  Pallas kernels  38.6 us (84%)
  local copies, waits for them, and re-layouts  5.93 us (13%)
  between operations  0.65 us (1%)
    pallas_call x1, Pallas kernels, body(): pl.pallas_call(functools.partial(kernel, n_dp, n_ctx, n_tp, cap), out_sha...  38.6 us
    unnamed x10, local copies, waits for them, and re-layouts  5.93 us

profile of v1, /device:TPU:1, one launch (start us, length us, event | category | flops | bytes accessed | tf_op | source)
XLA Modules:
  0.0 45.2 jit_solution(349103980674009645)
XLA Ops:
  0.6 38.6 %expert_layer.1 = (bf16[384,896]{1,0:T(8,128)(2,1)}, bf16[384,896]{1,0:T(8,128)(2,1)}, bf16[1,896,512]{2,1,0:T(8,128)(2,1)}, bf16[1,512,896]{2,1,0:T(8,128)(2,1)}) custom-call(s32[8,384]{1,0:T(8,128)} %bitcast.2, s32[8,384]{1,0:T(8,128)} %bitcast.3, bf16[384,896]{1,0:T(8,128)(2,1)} %tok_hbm.1, bf16[384,896]{1,0:T(8,128)(2,1)} %cot_hbm.1, ...), custom_call_target="tpu_custom_call" | custom-call | tf_op jit(solution)/shard_map/expert_layer/pallas_call | solution.py:256
  39.2 0.0 copy-start.2
  39.2 2.1 %copy.14 = bf16[384,896]{1,0:T(8,128)(2,1)} copy(bf16[384,896]{1,0:T(8,128)(2,1)} %get-tuple-element.8) | data formatting | bytes 1376256
  41.3 0.0 copy-done.2
  41.3 0.0 copy-start.1
  41.3 0.8 %copy.15 = bf16[384,896]{1,0:T(8,128)(2,1)} copy(bf16[384,896]{1,0:T(8,128)(2,1)S(1)} %copy-done.2) | data formatting | bytes 1376256
  42.2 0.6 %copy-done.1 = bf16[1,896,512]{2,1,0:T(8,128)(2,1)S(1)} copy-done((bf16[1,896,512]{2,1,0:T(8,128)(2,1)S(1)}, bf16[1,896,512]{2,1,0:T(8,128)(2,1)}, u32[]{:S(2)}) %copy-start.1) | copy-done | bytes 917528
  42.7 0.0 copy-start
  42.8 0.9 %copy.16 = bf16[1,896,512]{2,1,0:T(8,128)(2,1)} copy(bf16[1,896,512]{2,1,0:T(8,128)(2,1)S(1)} %copy-done.1) | data formatting | bytes 1835008
  43.7 0.6 %copy-done = bf16[1,512,896]{2,1,0:T(8,128)(2,1)S(1)} copy-done((bf16[1,512,896]{2,1,0:T(8,128)(2,1)S(1)}, bf16[1,512,896]{2,1,0:T(8,128)(2,1)}, u32[]{:S(2)}) %copy-start) | copy-done | bytes 917528
  44.3 0.9 %copy.17 = bf16[1,512,896]{2,1,0:T(8,128)(2,1)} copy(bf16[1,512,896]{2,1,0:T(8,128)(2,1)S(1)} %copy-done) | data formatting | bytes 1835008
Async XLA Ops:
  39.2 2.1 %copy-start.2 = (bf16[384,896]{1,0:T(8,128)(2,1)S(1)}, bf16[384,896]{1,0:T(8,128)(2,1)}, u32[]{:S(2)}) copy-start(bf16[384,896]{1,0:T(8,128)(2,1)} %get-tuple-element.9) | copy-start | bytes 2064388
  41.3 1.4 %copy-start.1 = (bf16[1,896,512]{2,1,0:T(8,128)(2,1)S(1)}, bf16[1,896,512]{2,1,0:T(8,128)(2,1)}, u32[]{:S(2)}) copy-start(bf16[1,896,512]{2,1,0:T(8,128)(2,1)} %get-tuple-element.10) | copy-start | bytes 2752516
  42.7 1.5 %copy-start = (bf16[1,512,896]{2,1,0:T(8,128)(2,1)S(1)}, bf16[1,512,896]{2,1,0:T(8,128)(2,1)}, u32[]{:S(2)}) copy-start(bf16[1,512,896]{2,1,0:T(8,128)(2,1)} %get-tuple-element.11) | copy-start | bytes 2752516

commit v2 on v1

v2 whole, which is shorter than its diff:
```python
import functools

import jax
import jax.numpy as jnp
from jax import lax
from jax.experimental import pallas as pl
from jax.experimental.pallas import tpu as pltpu
from jax.sharding import PartitionSpec as P

MESH = pl.DeviceIdType.MESH
F32 = jnp.float32
BF16 = jnp.bfloat16
FIRST = (((0,), (0,)), ((), ()))
LAST = (((1,), (1,)), ((), ()))
PLAIN = (((1,), (0,)), ((), ()))


def dot(a, b, how=PLAIN):
    return lax.dot_general(a, b, how, preferred_element_type=F32)


def kernel(
    n_dp, n_ctx, n_tp, cap,
    ids_ref, codes_ref, tok_hbm, cot_hbm, up_hbm, down_hbm,
    mixed, gtok, gup, gdown,
    tok, cot, up, down, x_send, g_send, x_recv, g_recv, x_all, g_all,
    h_send, a_send, h_recv, a_recv, act, ghid, act_all, ghid_all,
    p_send, q_send, p_recv, q_recv,
    in_sem, xs, xr, gs, gr, hs, hr, as_, ar, cs, cr, ds, dr, ps, pr, qs, qr,
):
    d, c, t = lax.axis_index("dp"), lax.axis_index("ctx"), lax.axis_index("tp")
    n_blocks = n_dp * n_ctx
    me = d * n_ctx + c
    slots = n_ctx * cap

    loads = [
        pltpu.make_async_copy(src, dst, in_sem.at[i])
        for i, (src, dst) in enumerate(
            ((tok_hbm, tok), (cot_hbm, cot), (up_hbm.at[0], up), (down_hbm.at[0], down))
        )
    ]
    for load in loads:
        load.start()

    def block_dev(k):
        b = lax.rem(me + k, n_blocks)
        return b, {"dp": b // n_ctx, "ctx": lax.rem(b, n_ctx)}

    def tp_dev(k):
        j = lax.rem(t + k, n_tp)
        return j, {"tp": j}

    barrier = pltpu.get_barrier_semaphore()
    for k in range(1, n_blocks):
        pl.semaphore_signal(barrier, inc=1, device_id=block_dev(k)[1], device_id_type=MESH)
    for k in range(1, n_tp):
        pl.semaphore_signal(barrier, inc=1, device_id=tp_dev(k)[1], device_id_type=MESH)

    picks, rows = ids_ref.shape
    lane = lax.broadcasted_iota(jnp.int32, (slots, rows), 0)
    lane_e = jnp.zeros((slots, rows), jnp.int32)
    for e in range(1, n_ctx):
        lane_e = lane_e + (lane >= e * cap).astype(jnp.int32)
    lane_s = lane - lane_e * cap
    named = jnp.zeros((slots, rows), jnp.int32)
    code = jnp.zeros((slots, rows), jnp.int32)
    ids, codes = ids_ref[...], codes_ref[...]
    for k in range(picks):
        hit = ids[k : k + 1] == lane_e
        named = jnp.where(hit, 1, named)
        code = jnp.where(hit, codes[k : k + 1], code)
    earlier = (
        lax.broadcasted_iota(jnp.int32, (rows, rows), 0)
        < lax.broadcasted_iota(jnp.int32, (rows, rows), 1)
    )
    rank = dot(named.astype(F32).astype(BF16), earlier.astype(F32).astype(BF16))
    chosen = jnp.where(rank == lane_s.astype(F32), named, 0)
    code = chosen * code
    pick = chosen.astype(F32).astype(BF16)
    high = lax.shift_right_logical(code, 8)
    gate_hi = (high.astype(F32) * (1.0 / 128.0)).astype(BF16)
    gate_lo = ((code - high * 256).astype(F32) * (1.0 / 32768.0)).astype(BF16)

    pl.semaphore_wait(barrier, n_blocks - 1 + n_tp - 1)

    def groups_dev(g, cc):
        return {"dp": g, "ctx": cc}

    def others(k):
        return range(1 if k == 0 else 0, n_ctx)

    def to(k, m):
        return lax.rem(d + k, n_dp), lax.rem(c + m, n_ctx)

    def spread(send, recv, send_sem, recv_sem, k, back=False):
        for m in others(k):
            g, e = to(k, m)
            src = send.at[g * n_ctx + e] if back else send.at[e]
            pltpu.make_async_remote_copy(
                src, recv.at[me], send_sem.at[k * n_ctx + m], recv_sem.at[me],
                device_id=groups_dev(g, e), device_id_type=MESH,
            ).start()
        if k == 0:
            recv[me] = send[me] if back else send[c]

    def arrived(recv, recv_sem, k):
        g = lax.rem(d + n_dp - k, n_dp)
        for m in others(k):
            e = lax.rem(c + m, n_ctx)
            b = g * n_ctx + e
            pltpu.make_async_remote_copy(
                recv.at[b], recv.at[b], recv_sem.at[b], recv_sem.at[b],
                device_id=groups_dev(g, e), device_id_type=MESH,
            ).wait_recv()
        return g

    def sent(send, send_sem):
        for k in range(n_dp):
            for m in others(k):
                g, e = to(k, m)
                i = k * n_ctx + m
                pltpu.make_async_remote_copy(
                    send.at[0], send.at[0], send_sem.at[i], send_sem.at[i],
                    device_id=groups_dev(g, e), device_id_type=MESH,
                ).wait_send()

    def put_blocks(ref, first, value, count):
        for b in range(count):
            ref[first + b] = value[b * cap : (b + 1) * cap].astype(BF16)

    def take_blocks(ref, first, count):
        return jnp.concatenate(
            [ref[first + b].astype(F32) for b in range(count)], axis=0
        ).astype(BF16)

    def tp_scatter(send, recv, send_sem, recv_sem, k):
        for m in range(1, n_tp):
            j, dev = tp_dev(m)
            pltpu.make_async_remote_copy(
                send.at[k, j], recv.at[k, t], send_sem.at[k, m], recv_sem.at[k, t],
                device_id=dev, device_id_type=MESH,
            ).start()

    def tp_gather(buf, send_sem, recv_sem, k):
        for m in range(1, n_tp):
            j, dev = tp_dev(m)
            pltpu.make_async_remote_copy(
                buf.at[k, t], buf.at[k, t], send_sem.at[k, m], recv_sem.at[k, t],
                device_id=dev, device_id_type=MESH,
            ).start()

    def tp_arrived(buf, recv_sem, k):
        for m in range(1, n_tp):
            j, dev = tp_dev(m)
            pltpu.make_async_remote_copy(
                buf.at[k, j], buf.at[k, j], recv_sem.at[k, j], recv_sem.at[k, j],
                device_id=dev, device_id_type=MESH,
            ).wait_recv()

    def tp_sent(buf, send_sem):
        for k in range(n_dp):
            for m in range(1, n_tp):
                j, dev = tp_dev(m)
                pltpu.make_async_remote_copy(
                    buf.at[k, 0], buf.at[k, 0], send_sem.at[k, m], send_sem.at[k, m],
                    device_id=dev, device_id_type=MESH,
                ).wait_send()

    forth, back = list(range(n_dp)), list(reversed(range(n_dp)))
    loads[0].wait()
    put_blocks(x_send, 0, dot(pick, tok[...]), n_ctx)
    for k in forth:
        spread(x_send, x_recv, xs, xr, k)
    loads[1].wait()
    put_blocks(g_send, 0, dot(gate_hi, cot[...]) + dot(gate_lo, cot[...]), n_ctx)
    for k in back:
        spread(g_send, g_recv, gs, gr, k)

    group = slots
    piece = group // n_tp

    def put_pieces(ref, k, value):
        for j in range(n_tp):
            ref[k, j] = value[j * piece : (j + 1) * piece].astype(BF16)

    def total(send, recv, k):
        value = send[k, t].astype(F32)
        for m in range(1, n_tp):
            value = value + recv[k, lax.rem(t + m, n_tp)].astype(F32)
        return value

    loads[2].wait()
    for k in forth:
        g = arrived(x_recv, xr, k)
        x_all[k * group : (k + 1) * group] = take_blocks(x_recv, g * n_ctx, n_ctx)
        put_pieces(h_send, k, dot(x_all[k * group : (k + 1) * group], up[...]))
        tp_scatter(h_send, h_recv, hs, hr, k)
    loads[3].wait()
    for k in back:
        g = arrived(g_recv, gr, k)
        g_all[k * group : (k + 1) * group] = take_blocks(g_recv, g * n_ctx, n_ctx)
        put_pieces(a_send, k, dot(g_all[k * group : (k + 1) * group], down[...], LAST))
        tp_scatter(a_send, a_recv, as_, ar, k)

    for k in back:
        tp_arrived(h_recv, hr, k)
        hidden = total(h_send, h_recv, k)
        sigma = 1.0 / (1.0 + jnp.exp(-hidden))
        act[k, t] = (hidden * sigma).astype(BF16)
        tp_gather(act, cs, cr, k)
        slope = sigma * (1.0 + hidden * (1.0 - sigma))
        tp_arrived(a_recv, ar, k)
        ghid[k, t] = (total(a_send, a_recv, k) * slope).astype(BF16)
        tp_gather(ghid, ds, dr, k)

    def whole(buf, k):
        return jnp.concatenate([buf[k, j].astype(F32) for j in range(n_tp)], axis=0).astype(BF16)

    for k in back:
        rows_k = slice(k * group, (k + 1) * group)
        first = lax.rem(d + n_dp - k, n_dp) * n_ctx
        to_k = (n_dp - k) % n_dp
        tp_arrived(act, cr, k)
        act_all[rows_k] = whole(act, k)
        put_blocks(p_send, first, dot(act_all[rows_k], down[...]), n_ctx)
        spread(p_send, p_recv, ps, pr, to_k, back=True)
        tp_arrived(ghid, dr, k)
        ghid_all[rows_k] = whole(ghid, k)
        put_blocks(q_send, first, dot(ghid_all[rows_k], up[...], LAST), n_ctx)
        spread(q_send, q_recv, qs, qr, to_k, back=True)

    gdown[0] = dot(act_all[...], g_all[...], FIRST).astype(BF16)
    gup[0] = dot(x_all[...], ghid_all[...], FIRST).astype(BF16)

    for k in back:
        arrived(p_recv, pr, k)
    out = jnp.zeros(mixed.shape, F32)
    for g in range(n_dp):
        got = take_blocks(p_recv, g * n_ctx, n_ctx)
        out = out + dot(gate_hi, got, FIRST) + dot(gate_lo, got, FIRST)
    mixed[...] = out.astype(BF16)
    for k in back:
        arrived(q_recv, qr, k)
    out = jnp.zeros(gtok.shape, F32)
    for g in range(n_dp):
        out = out + dot(pick, take_blocks(q_recv, g * n_ctx, n_ctx), FIRST)
    gtok[...] = out.astype(BF16)

    sent(x_send, xs)
    sent(g_send, gs)
    tp_sent(h_recv, hs)
    tp_sent(a_recv, as_)
    tp_sent(act, cs)
    tp_sent(ghid, ds)
    sent(p_send, ps)
    sent(q_send, qs)


def store(*refs):
    sem = refs[-1]
    copies = [
        pltpu.make_async_copy(src, dst, sem.at[i])
        for i, (src, dst) in enumerate(zip(refs[:4], refs[4:8]))
    ]
    for copy in copies:
        copy.start()
    for copy in copies:
        copy.wait()


def body(n_dp, n_ctx, n_tp, tokens, expert_ids, gate_codes, up_weight, down_weight, cotangent):
    rows, feats = tokens.shape
    hid = up_weight.shape[2]
    cap = rows // 16
    blocks = n_dp * n_ctx
    total = blocks * cap
    piece = n_ctx * cap // n_tp
    any_ = pl.BlockSpec(memory_space=pl.ANY)
    vmem = pl.BlockSpec(memory_space=pltpu.VMEM)
    dma = pltpu.SemaphoreType.DMA

    def buf(*shape):
        return pltpu.VMEM(shape, BF16)

    tp_sems = [dma((n_dp, n_tp))] * 8
    results = pl.pallas_call(
        functools.partial(kernel, n_dp, n_ctx, n_tp, cap),
        out_shape=[
            buf(*a.shape) for a in (tokens, tokens, up_weight, down_weight)
        ],
        in_specs=[vmem, vmem, any_, any_, any_, any_],
        out_specs=[vmem] * 4,
        scratch_shapes=[
            buf(rows, feats), buf(rows, feats), buf(feats, hid), buf(hid, feats),
            buf(n_ctx, cap, feats), buf(n_ctx, cap, feats),
            buf(blocks, cap, feats), buf(blocks, cap, feats),
            buf(total, feats), buf(total, feats),
            buf(n_dp, n_tp, piece, hid), buf(n_dp, n_tp, piece, hid),
            buf(n_dp, n_tp, piece, hid), buf(n_dp, n_tp, piece, hid),
            buf(n_dp, n_tp, piece, hid), buf(n_dp, n_tp, piece, hid),
            buf(total, hid), buf(total, hid),
            buf(blocks, cap, feats), buf(blocks, cap, feats),
            buf(blocks, cap, feats), buf(blocks, cap, feats),
            dma((4,)),
            dma((blocks,)), dma((blocks,)), dma((blocks,)), dma((blocks,)),
            *tp_sems,
            dma((blocks,)), dma((blocks,)), dma((blocks,)), dma((blocks,)),
        ],
        compiler_params=pltpu.CompilerParams(
            collective_id=0, has_side_effects=True, vmem_limit_bytes=58 * 2**20
        ),
        name="expert_layer",
    )(expert_ids.T, gate_codes.T, tokens, cotangent, up_weight, down_weight)
    return tuple(
        pl.pallas_call(
            store,
            out_shape=[
                jax.ShapeDtypeStruct(a.shape, BF16)
                for a in (tokens, tokens, up_weight, down_weight)
            ],
            in_specs=[vmem] * 4,
            out_specs=[any_] * 4,
            scratch_shapes=[dma((4,))],
            compiler_params=pltpu.CompilerParams(vmem_limit_bytes=2**20),
            name="store",
        )(*[pltpu.with_memory_space_constraint(a, pltpu.VMEM) for a in results])
    )


def solution(mesh):
    sizes = [mesh.shape[name] for name in ("dp", "ctx", "tp")]
    return jax.shard_map(
        functools.partial(body, *sizes),
        mesh=mesh,
        in_specs=(
            P(("dp", "ctx"), "tp"),
            P(("dp", "ctx"), None),
            P(("dp", "ctx"), None),
            P("ctx", "tp", "dp"),
            P("ctx", "dp", "tp"),
            P(("dp", "ctx"), "tp"),
        ),
        out_specs=(
            P(("dp", "ctx"), "tp"),
            P(("dp", "ctx"), "tp"),
            P("ctx", "tp", "dp"),
            P("ctx", "dp", "tp"),
        ),
        check_vma=False,
    )
```

time: 45.8 us -> 40.8 us (0.89)
  local copies, waits for them, and re-layouts: 5.93 us -> 0 us
  Pallas kernels: 38.6 us -> 39.8 us
    unnamed x10 -> x0, local copies, waits for them, and re-layouts: 5.93 us -> none
    pallas_call x0 -> x1, Pallas kernels: none -> 1.72 us  [body(): pl.pallas_call(store, out_shape=[jax.ShapeDtypeStruct(a.shape, BF16) for...]
    pallas_call x1, Pallas kernels: 38.6 us -> 38.1 us  [body(): pl.pallas_call(functools.partial(kernel, n_dp, n_ctx, n_tp, cap), out_sha...]
where the time goes in v2:
time: 40.8 us; the launch traced here: 40.5 us
  Pallas kernels  39.8 us (98%)
  between operations  0.64 us (2%)
    pallas_call x1, Pallas kernels, body(): pl.pallas_call(functools.partial(kernel, n_dp, n_ctx, n_tp, cap), out_sha...  38.1 us
    pallas_call x1, Pallas kernels, body(): pl.pallas_call(store, out_shape=[jax.ShapeDtypeStruct(a.shape, BF16) for...  1.72 us

profile of v2, /device:TPU:1, one launch (start us, length us, event | category | flops | bytes accessed | tf_op | source)
XLA Modules:
  0.0 40.5 jit_solution(7579234769174579792)
XLA Ops:
  0.6 38.1 %expert_layer.1 = (bf16[384,896]{1,0:T(8,128)(2,1)S(1)}, bf16[384,896]{1,0:T(8,128)(2,1)S(1)}, bf16[1,896,512]{2,1,0:T(8,128)(2,1)S(1)}, bf16[1,512,896]{2,1,0:T(8,128)(2,1)S(1)}) custom-call(s32[8,384]{1,0:T(8,128)} %bitcast.2, s32[8,384]{1,0:T(8,128)} %bitcast.3, bf16[384,896]{1,0:T(8,128)(2,1)} %tok_hbm.1, bf16[384,896]{1,0:T(8,128)(2,1)} %cot_hbm.1, ...), custom_call_target="tpu_custom_call" | custom-call | tf_op jit(solution)/shard_map/expert_layer/pallas_call | solution.py:286
  38.8 1.7 %store.1 = (bf16[384,896]{1,0:T(8,128)(2,1)}, bf16[384,896]{1,0:T(8,128)(2,1)}, bf16[1,896,512]{2,1,0:T(8,128)(2,1)}, bf16[1,512,896]{2,1,0:T(8,128)(2,1)}) custom-call(bf16[384,896]{1,0:T(8,128)(2,1)S(1)} %get-tuple-element.8.refs_0_, bf16[384,896]{1,0:T(8,128)(2,1)S(1)} %get-tuple-element.9.refs_1_, bf16[1,896,512]{2,1,0:T(8,128)(2,1)S(1)} %get-tuple-element.10.refs_2_, ...), custom_call_target="tpu_custom_call" | custom-call | tf_op jit(solution)/shard_map/store/pallas_call | solution.py:315

commit v3 on v2

--- a/solution.py
+++ b/solution.py
@@ -81,8 +81,6 @@
     gate_hi = (high.astype(F32) * (1.0 / 128.0)).astype(BF16)
     gate_lo = ((code - high * 256).astype(F32) * (1.0 / 32768.0)).astype(BF16)
 
-    pl.semaphore_wait(barrier, n_blocks - 1 + n_tp - 1)
-
     def groups_dev(g, cc):
         return {"dp": g, "ctx": cc}
 
@@ -169,6 +167,7 @@
     forth, back = list(range(n_dp)), list(reversed(range(n_dp)))
     loads[0].wait()
     put_blocks(x_send, 0, dot(pick, tok[...]), n_ctx)
+    pl.semaphore_wait(barrier, n_blocks - 1 + n_tp - 1)
     for k in forth:
         spread(x_send, x_recv, xs, xr, k)
     loads[1].wait()
@@ -195,35 +194,41 @@
         x_all[k * group : (k + 1) * group] = take_blocks(x_recv, g * n_ctx, n_ctx)
         put_pieces(h_send, k, dot(x_all[k * group : (k + 1) * group], up[...]))
         tp_scatter(h_send, h_recv, hs, hr, k)
-    loads[3].wait()
-    for k in back:
-        g = arrived(g_recv, gr, k)
-        g_all[k * group : (k + 1) * group] = take_blocks(g_recv, g * n_ctx, n_ctx)
-        put_pieces(a_send, k, dot(g_all[k * group : (k + 1) * group], down[...], LAST))
-        tp_scatter(a_send, a_recv, as_, ar, k)
-
-    for k in back:
+    slopes = [None] * n_dp
+    for k in forth:
         tp_arrived(h_recv, hr, k)
         hidden = total(h_send, h_recv, k)
         sigma = 1.0 / (1.0 + jnp.exp(-hidden))
         act[k, t] = (hidden * sigma).astype(BF16)
         tp_gather(act, cs, cr, k)
-        slope = sigma * (1.0 + hidden * (1.0 - sigma))
-        tp_arrived(a_recv, ar, k)
-        ghid[k, t] = (total(a_send, a_recv, k) * slope).astype(BF16)
-        tp_gather(ghid, ds, dr, k)
+        slopes[k] = sigma * (1.0 + hidden * (1.0 - sigma))
+    loads[3].wait()
+    for k in back:
+        g = arrived(g_recv, gr, k)
+        g_all[k * group : (k + 1) * group] = take_blocks(g_recv, g * n_ctx, n_ctx)
+        put_pieces(a_send, k, dot(g_all[k * group : (k + 1) * group], down[...], LAST))
+        tp_scatter(a_send, a_recv, as_, ar, k)
 
     def whole(buf, k):
         return jnp.concatenate([buf[k, j].astype(F32) for j in range(n_tp)], axis=0).astype(BF16)
 
+    def home(k):
+        return lax.rem(d + n_dp - k, n_dp) * n_ctx, (n_dp - k) % n_dp
+
     for k in back:
         rows_k = slice(k * group, (k + 1) * group)
-        first = lax.rem(d + n_dp - k, n_dp) * n_ctx
-        to_k = (n_dp - k) % n_dp
+        first, to_k = home(k)
         tp_arrived(act, cr, k)
         act_all[rows_k] = whole(act, k)
         put_blocks(p_send, first, dot(act_all[rows_k], down[...]), n_ctx)
         spread(p_send, p_recv, ps, pr, to_k, back=True)
+    for k in back:
+        tp_arrived(a_recv, ar, k)
+        ghid[k, t] = (total(a_send, a_recv, k) * slopes[k]).astype(BF16)
+        tp_gather(ghid, ds, dr, k)
+    for k in back:
+        rows_k = slice(k * group, (k + 1) * group)
+        first, to_k = home(k)
         tp_arrived(ghid, dr, k)
         ghid_all[rows_k] = whole(ghid, k)
         put_blocks(q_send, first, dot(ghid_all[rows_k], up[...], LAST), n_ctx)

time: 40.8 us -> 40.4 us (level)
  no operation moved by 1% of the time
where the time goes in v3:
time: 40.4 us; the launch traced here: 40.1 us
  Pallas kernels  39.5 us (98%)
  between operations  0.64 us (2%)
    pallas_call x1, Pallas kernels, body(): pl.pallas_call(functools.partial(kernel, n_dp, n_ctx, n_tp, cap), out_sha...  37.8 us
    pallas_call x1, Pallas kernels, body(): pl.pallas_call(store, out_shape=[jax.ShapeDtypeStruct(a.shape, BF16) for...  1.72 us

profile of v3, /device:TPU:1, one launch (start us, length us, event | category | flops | bytes accessed | tf_op | source)
XLA Modules:
  0.0 40.1 jit_solution(4266767326076653840)
XLA Ops:
  0.6 37.8 %expert_layer.1 = (bf16[384,896]{1,0:T(8,128)(2,1)S(1)}, bf16[384,896]{1,0:T(8,128)(2,1)S(1)}, bf16[1,896,512]{2,1,0:T(8,128)(2,1)S(1)}, bf16[1,512,896]{2,1,0:T(8,128)(2,1)S(1)}) custom-call(s32[8,384]{1,0:T(8,128)} %bitcast.2, s32[8,384]{1,0:T(8,128)} %bitcast.3, bf16[384,896]{1,0:T(8,128)(2,1)} %tok_hbm.1, bf16[384,896]{1,0:T(8,128)(2,1)} %cot_hbm.1, ...), custom_call_target="tpu_custom_call" | custom-call | tf_op jit(solution)/shard_map/expert_layer/pallas_call | solution.py:291
  38.4 1.7 %store.1 = (bf16[384,896]{1,0:T(8,128)(2,1)}, bf16[384,896]{1,0:T(8,128)(2,1)}, bf16[1,896,512]{2,1,0:T(8,128)(2,1)}, bf16[1,512,896]{2,1,0:T(8,128)(2,1)}) custom-call(bf16[384,896]{1,0:T(8,128)(2,1)S(1)} %get-tuple-element.8.refs_0_, bf16[384,896]{1,0:T(8,128)(2,1)S(1)} %get-tuple-element.9.refs_1_, bf16[1,896,512]{2,1,0:T(8,128)(2,1)S(1)} %get-tuple-element.10.refs_2_, ...), custom_call_target="tpu_custom_call" | custom-call | tf_op jit(solution)/shard_map/store/pallas_call | solution.py:320
